TPU v7x, 512 devices: a whole 4x4x16 slice. The times are simulated.
512 devices in a mesh: user: 64 (over y, x, z_hi, core), isec: 8 (over z_lo).
Axes of the slice: x: 4, y: 4, z: 16 (z_hi: 2, z_lo: 8; z = z_hi * 8 + z_lo), core: 2. Of those that a mesh axis runs over, the one named last changes fastest.
Arguments:
- user_factors: float32 [32768, 512], P('user'), may hold values from -1.5 to 1.5
- item_factors: float32 [131072, 512], P(('user', 'isec')), may hold values from -1.5 to 1.5
- confidence: bfloat16 [64, 8, 4, 6, 128, 128], P('user', 'isec'), may hold values from 0.19921875 to 5
- tile_ids: int32 [64, 8, 4, 6], P('user', 'isec'), may hold values from 0 to 7, as said below
- tile_counts: int32 [64, 8, 4], P('user', 'isec'), may hold values from 1 to 6, as said below
Outputs:
- new_user_factors: float32 [32768, 512], P(('user', 'isec'))
- new_item_factors: float32 [131072, 512], P(('user', 'isec'))
Inputs may be any that keep to these rules, and one draw needn't show every extreme that they name: `tile_ids`: the 6 positions of one list name different tiles. `tile_counts`: some list has all 6 positions live.
All inputs are finite; a program needn't handle non-finite values.
Results may differ from a plain program's by a relative error of at most 0.0003.
Values sent between devices are 32-bit elements; how exact they have to be, the bound alone decides.
A program may use at most 64 MiB of HBM per device.

v0:
```python
import functools

import jax
import jax.numpy as jnp
from jax import lax
from jax.experimental import pallas as pl
from jax.experimental.pallas import tpu as pltpu
from jax.sharding import PartitionSpec as P

TILE = 128
VISITS = 4

item_rate = 0.02
user_rate = 0.005
shrinkage = 0.1

MESH = pl.DeviceIdType.MESH
F32 = jnp.float32
BF16 = jnp.bfloat16


def halves(value):
    high = value.astype(BF16)
    low = (value - high.astype(F32)).astype(BF16)
    return high, low


def dot3(left, right, dims):
    one = functools.partial(
        lax.dot_general, dimension_numbers=(dims, ((), ())), preferred_element_type=F32
    )
    return one(left[0], right[0]) + (one(left[0], right[1]) + one(left[1], right[0]))


def kernel(
    n_user, n_isec,
    ids_ref, counts_ref, p_hbm, q_hbm, c_hbm,
    users_ref, items_ref,
    p_v, p_hi, p_lo, q_in, q_out, q_hi, q_lo, c_v, et_hi, et_lo, e_hi, e_lo,
    g_v, g_peer, runs, fin_out, fin_in,
    load_sem, send_sem, recv_sem, g_send, g_recv, run_send, run_recv, fin_send, fin_recv,
):
    user_rows, rank = p_v.shape
    block = q_in.shape[1]
    user_tiles = user_rows // TILE
    item_tiles = block // TILE
    share = user_rows // n_isec
    last = n_isec - 1

    u = lax.axis_index("user")
    s = lax.axis_index("isec")
    core = lax.rem(u, 2)
    nxt = lax.rem(u + 1, n_user)
    prv = lax.rem(u + n_user - 1, n_user)
    home = lax.rem(u + n_user - (VISITS - 1), n_user)
    guest = lax.rem(u + VISITS - 1, n_user)

    load_p = pltpu.make_async_copy(p_hbm, p_v, load_sem.at[0])
    load_q = pltpu.make_async_copy(q_hbm, q_in.at[0], load_sem.at[1])
    load_c = pltpu.make_async_copy(c_hbm, c_v, load_sem.at[2])
    load_p.start()
    load_q.start()
    load_c.start()

    barrier = pltpu.get_barrier_semaphore()
    for other in (nxt, prv, home, guest):
        pl.semaphore_signal(
            barrier, inc=1, device_id={"user": other}, device_id_type=MESH
        )

    @pl.when((core == 0) & (s > 0))
    def _():
        pl.semaphore_signal(
            barrier, inc=1, device_id={"isec": s - 1}, device_id_type=MESH
        )

    @pl.when((core == 0) & (s < last))
    def _():
        pl.semaphore_signal(
            barrier, inc=1, device_id={"isec": s + 1}, device_id_type=MESH
        )

    load_p.wait()
    for i in range(user_tiles):
        rows = pl.ds(i * TILE, TILE)
        high, low = halves(p_v[rows, :])
        p_hi[rows, :] = high
        p_lo[rows, :] = low
    load_q.wait()
    load_c.wait()

    def errors(visit):
        high, low = halves(q_in[visit])
        q_hi[...] = high
        q_lo[...] = low
        for i in range(user_tiles):
            rows = pl.ds(i * TILE, TILE)
            x = dot3(
                (p_hi[rows, :], p_lo[rows, :]), (q_hi[...], q_lo[...]), ((1,), (1,))
            )
            for j in range(item_tiles):
                k = i * item_tiles + j
                place = jnp.int32(0)
                live = jnp.int32(0)
                for n in range(c_v.shape[1]):
                    hit = (ids_ref[visit, n] == k) & (n < counts_ref[visit])
                    place = place + jnp.where(hit, n, 0)
                    live = live + jnp.where(hit, 1, 0)
                columns = slice(j * TILE, (j + 1) * TILE)
                weight = c_v[visit, place].astype(F32)
                e = jnp.where(live > 0, weight * (x[:, columns] - 1.0), 0.0)
                high, low = halves(e)
                e_hi[rows, pl.ds(j * TILE, TILE)] = high
                e_lo[rows, pl.ds(j * TILE, TILE)] = low
                high, low = halves(e.T)
                et_hi[pl.ds(j * TILE, TILE), rows] = high
                et_lo[pl.ds(j * TILE, TILE), rows] = low

    def item_step(visit):
        for j in range(item_tiles):
            rows = pl.ds(j * TILE, TILE)
            d = dot3(
                (et_hi[rows, :], et_lo[rows, :]), (p_hi[...], p_lo[...]), ((1,), (0,))
            )
            q = q_in[visit, rows, :]
            q_out[visit, rows, :] = q - item_rate * (d + shrinkage * q)

    def user_step(visit):
        for i in range(user_tiles):
            rows = pl.ds(i * TILE, TILE)
            g = dot3(
                (e_hi[rows, :], e_lo[rows, :]), (q_hi[...], q_lo[...]), ((1,), (0,))
            )
            if visit == 0:
                g_v[rows, :] = g
            else:
                g_v[rows, :] = g_v[rows, :] + g

    def moved(visit):
        if visit < VISITS - 1:
            target, place = nxt, q_in.at[visit + 1]
        else:
            target, place = home, items_ref
        return pltpu.make_async_remote_copy(
            src_ref=q_out.at[visit],
            dst_ref=place,
            send_sem=send_sem.at[visit],
            recv_sem=recv_sem.at[visit],
            device_id={"user": target},
            device_id_type=MESH,
        )

    def gradient_over(other):
        return pltpu.make_async_remote_copy(
            src_ref=g_v,
            dst_ref=g_peer,
            send_sem=g_send,
            recv_sem=g_recv,
            device_id={"user": other},
            device_id_type=MESH,
        )

    def run_copy(who, way, d, source, target):
        return pltpu.make_async_remote_copy(
            src_ref=source,
            dst_ref=runs.at[who, way, d],
            send_sem=run_send.at[who, way, d],
            recv_sem=run_recv.at[who, way, d],
            device_id={"isec": target},
            device_id_type=MESH,
        )

    def shard(ref, d):
        return ref.at[pl.ds(pl.multiple_of(d * share, share), share), :]

    def reduce_line(who, g_ref):
        def step(t, carry):
            d = last + s - t

            @pl.when(t >= s)
            def _():
                @pl.when(s > 0)
                def _():
                    run_copy(who, 0, d, runs.at[who, 0, d], s).wait_recv()

                @pl.when((d > s) & (s > 0))
                def _():
                    runs[who, 0, d] = runs[who, 0, d] + shard(g_ref, d)[...]
                    run_copy(who, 0, d, runs.at[who, 0, d], s + 1).start()

                @pl.when((d > s) & (s == 0))
                def _():
                    run_copy(who, 0, d, shard(g_ref, d), s + 1).start()

            b = t - last + s

            @pl.when(t >= last - s)
            def _():
                @pl.when(s < last)
                def _():
                    run_copy(who, 1, b, runs.at[who, 1, b], s).wait_recv()

                @pl.when((b < s) & (s < last))
                def _():
                    runs[who, 1, b] = runs[who, 1, b] + shard(g_ref, b)[...]
                    run_copy(who, 1, b, runs.at[who, 1, b], s - 1).start()

                @pl.when((b < s) & (s == last))
                def _():
                    run_copy(who, 1, b, shard(g_ref, b), s - 1).start()

            return carry

        lax.fori_loop(0, n_isec, step, 0)

    def line_total(who, g_ref):
        mine = shard(g_ref, s)[...]
        right = jnp.where(s > 0, runs[who, 0, s], 0.0)
        left = jnp.where(s < last, runs[who, 1, s], 0.0)
        return mine + (right + left)

    def drain_line(who, g_ref):
        def step(d, carry):
            @pl.when(d > s)
            def _():
                run_copy(who, 0, d, runs.at[who, 0, d], s).wait_send()

            @pl.when(d < s)
            def _():
                run_copy(who, 1, d, runs.at[who, 1, d], s).wait_send()

            return carry

        lax.fori_loop(0, n_isec, step, 0)

    def finish(total):
        own = p_v[pl.ds(pl.multiple_of(s * share, share), share), :]
        users_ref[...] = own - user_rate * (total + shrinkage * own)

    def finish_copy(other):
        return pltpu.make_async_remote_copy(
            src_ref=fin_out,
            dst_ref=fin_in,
            send_sem=fin_send,
            recv_sem=fin_recv,
            device_id={"user": other},
            device_id_type=MESH,
        )

    for visit in range(VISITS):
        if visit > 0:
            moved(visit - 1).wait_recv()
        errors(visit)
        if visit == 0:
            item_step(visit)
            greeted = jnp.where(s > 0, 1, 0) + jnp.where(s < last, 1, 0)
            pl.semaphore_wait(barrier, 4 + jnp.where(core == 0, greeted, 0))
            moved(visit).start()
            user_step(visit)
        elif visit < VISITS - 1:
            item_step(visit)
            moved(visit).start()
            user_step(visit)
        else:
            user_step(visit)

            @pl.when(core == 1)
            def _():
                gradient_over(prv).start()

            item_step(visit)
            moved(visit).start()

        if visit == VISITS - 2:

            @pl.when(core == 0)
            def _():
                gradient_over(prv).wait_recv()
                reduce_line(0, g_peer)
                fin_out[...] = line_total(0, g_peer)
                finish_copy(nxt).start()

    @pl.when(core == 0)
    def _():
        reduce_line(1, g_v)
        finish(line_total(1, g_v))
        drain_line(0, g_peer)
        drain_line(1, g_v)
        finish_copy(nxt).wait_send()

    @pl.when(core == 1)
    def _():
        gradient_over(prv).wait_send()
        finish_copy(nxt).wait_recv()
        finish(fin_in[...])

    for visit in range(VISITS):
        moved(visit).wait_send()
    moved(VISITS - 1).wait_recv()


def on_device(n_user, n_isec, user_factors, item_factors, confidence, tile_ids, tile_counts):
    user_rows, rank = user_factors.shape
    block = item_factors.shape[0]
    tiles = confidence.shape[3]
    share = user_rows // n_isec
    vmem = functools.partial(pltpu.VMEM, dtype=F32)
    dma = pltpu.SemaphoreType.DMA
    return pl.pallas_call(
        functools.partial(kernel, n_user, n_isec),
        out_shape=(
            jax.ShapeDtypeStruct((share, rank), F32),
            jax.ShapeDtypeStruct((block, rank), F32),
        ),
        in_specs=[pl.BlockSpec(memory_space=pltpu.SMEM)] * 2
        + [pl.BlockSpec(memory_space=pl.ANY)] * 3,
        out_specs=(
            pl.BlockSpec(memory_space=pltpu.VMEM),
            pl.BlockSpec(memory_space=pl.ANY),
        ),
        scratch_shapes=[
            vmem((user_rows, rank)),
            pltpu.VMEM((user_rows, rank), BF16),
            pltpu.VMEM((user_rows, rank), BF16),
            vmem((VISITS, block, rank)),
            vmem((VISITS, block, rank)),
            pltpu.VMEM((block, rank), BF16),
            pltpu.VMEM((block, rank), BF16),
            pltpu.VMEM((VISITS, tiles, TILE, TILE), BF16),
            pltpu.VMEM((block, user_rows), BF16),
            pltpu.VMEM((block, user_rows), BF16),
            pltpu.VMEM((user_rows, block), BF16),
            pltpu.VMEM((user_rows, block), BF16),
            vmem((user_rows, rank)),
            vmem((user_rows, rank)),
            vmem((2, 2, n_isec, share, rank)),
            vmem((share, rank)),
            vmem((share, rank)),
            dma((3,)),
            dma((VISITS,)),
            dma((VISITS,)),
            dma,
            dma,
            dma((2, 2, n_isec)),
            dma((2, 2, n_isec)),
            dma,
            dma,
        ],
        compiler_params=pltpu.CompilerParams(
            collective_id=0, has_side_effects=True
        ),
        name="window",
    )(tile_ids[0, 0], tile_counts[0, 0], user_factors, item_factors, confidence[0, 0])


def solution(mesh):
    sizes = dict(mesh.shape)
    return jax.shard_map(
        functools.partial(on_device, sizes["user"], sizes["isec"]),
        mesh=mesh,
        in_specs=(
            P("user", None),
            P(("user", "isec"), None),
            P("user", "isec", None, None, None, None),
            P("user", "isec", None, None),
            P("user", "isec", None),
        ),
        out_specs=(P(("user", "isec"), None), P(("user", "isec"), None)),
        check_vma=False,
    )
```

profile of v0, /device:TPU:290, one launch (start us, length us, event | category | flops | bytes accessed | tf_op | source)
XLA Modules:
  0.0 170.4 jit_solution(6923612688189839463)
XLA Ops:
  0.6 166.4 %window.1 = (f32[64,512]{1,0:T(8,128)}, f32[256,512]{1,0:T(8,128)}) custom-call(s32[4,6]{1,0:T(4,128)} %bitcast.4, s32[4]{0:T(128)} %bitcast.5, f32[512,512]{1,0:T(8,128)} %p_hbm.1, f32[256,512]{1,0:T(8,128)} %q_hbm.1, bf16[4,6,128,128]{3,2,1,0:T(8,128)(2,1)} %bitcast.3), custom_call_target="tpu_custom_call" | custom-call | tf_op jit(solution)/shard_map/window/pallas_call | solution.py:309
  167.0 1.6 copy.9
  168.6 1.9 %copy.10 = f32[256,512]{1,0:T(8,128)} copy(f32[256,512]{1,0:T(8,128)} %get-tuple-element.5) | data formatting | bytes 1048576
where the time goes:
time: 171 us; the launch traced here: 170 us
  Pallas kernels  166 us (97%)
  local copies, waits for them, and re-layouts  3.44 us (2%)
    pallas_call x1, Pallas kernels, on_device(): pl.pallas_call(functools.partial(kernel, n_user, n_isec), out_shape=(jax....  166 us
    unnamed x2, local copies, waits for them, and re-layouts  3.44 us

commit v1 on v0

v1 whole, which is shorter than its diff:
```python
import functools

import jax
import jax.numpy as jnp
from jax import lax
from jax.experimental import pallas as pl
from jax.experimental.pallas import tpu as pltpu
from jax.sharding import PartitionSpec as P

TILE = 128
VISITS = 4
CHUNKS = 4
PARTS = 2
LEAD = 3

item_rate = 0.02
user_rate = 0.005
shrinkage = 0.1

MESH = pl.DeviceIdType.MESH
F32 = jnp.float32
BF16 = jnp.bfloat16


def halves(value):
    high = value.astype(BF16)
    low = (value - high.astype(F32)).astype(BF16)
    return high, low


def dot3(left, right, dims):
    one = functools.partial(
        lax.dot_general, dimension_numbers=(dims, ((), ())), preferred_element_type=F32
    )
    return one(left[0], right[0]) + (one(left[0], right[1]) + one(left[1], right[0]))


def kernel(
    n_user, n_isec,
    ids_ref, counts_ref, p_hbm, q_hbm, c_hbm,
    users_ref, items_ref,
    p_v, p_hi, p_lo, q_in, q_out, q_hi, q_lo, c_v, et_hi, et_lo, e_hi, e_lo,
    g_v, g_peer, runs, fin_out, fin_in, relay,
    load_sem, near_send, near_recv, far_send, hop_recv, far_recv,
    g_send, g_recv, run_send, run_recv, fin_send, fin_recv,
):
    user_rows, rank = p_v.shape
    block = q_in.shape[1]
    user_tiles = user_rows // TILE
    item_tiles = block // TILE
    share = user_rows // n_isec
    last = n_isec - 1

    ring = 2 * n_isec
    chunks = hop_recv.shape[3]
    chunk_rows = block // 2 // chunks

    u = lax.axis_index("user")
    s = lax.axis_index("isec")
    core = lax.rem(u, 2)
    column = u // 4
    z = lax.rem(u // 2, 2) * n_isec + s
    nxt = lax.rem(u + 1, n_user)
    prv = lax.rem(u + n_user - 1, n_user)
    home = lax.rem(u + n_user - (VISITS - 1), n_user)
    guest = lax.rem(u + VISITS - 1, n_user)
    way_step = (1, ring - 1)

    def owner(col, z_at, at_core):
        return (col * 2 + z_at // n_isec) * 2 + at_core

    def chip(col, z_at, at_core):
        z_at = lax.rem(z_at, ring)
        return {"user": owner(col, z_at, at_core), "isec": lax.rem(z_at, n_isec)}

    def shift_of(visit):
        return 1 if visit < VISITS - 1 else n_user - (VISITS - 1)

    def relay_target(way, visit):
        source = lax.rem(z + (ring - way_step[way]) * (n_isec - 1), ring)
        first = owner(column, source, 1)
        return {
            "user": lax.rem(first + shift_of(visit), n_user),
            "isec": lax.rem(source, n_isec),
        }

    def relay_origin(way, visit):
        first = lax.rem(u + n_user - shift_of(visit), n_user)
        return chip(first // 4, z + ring - way_step[way], 1)

    load_q = pltpu.make_async_copy(q_hbm, q_in.at[0], load_sem.at[user_tiles])
    load_c = pltpu.make_async_copy(c_hbm, c_v, load_sem.at[user_tiles + 1])

    def load_p(i):
        rows = pl.ds(i * TILE, TILE)
        return pltpu.make_async_copy(p_hbm.at[rows, :], p_v.at[rows, :], load_sem.at[i])

    for i in range(user_tiles):
        load_p(i).start()
    load_q.start()
    load_c.start()

    barrier = pltpu.get_barrier_semaphore()

    def greet(device):
        pl.semaphore_signal(barrier, inc=1, device_id=device, device_id_type=MESH)

    @pl.when(core == 1)
    def _():
        for way in range(2):
            greet(chip(column, z + way_step[way], 1))
            greet(relay_target(way, 0))
            greet(relay_target(way, VISITS - 1))
        greet({"user": prv})
        greet({"user": guest})

    @pl.when(core == 0)
    def _():
        for way in range(2):
            greet(relay_origin(way, 0))
            greet(relay_origin(way, VISITS - 1))
        greet({"user": nxt})
        greet({"user": home})

    @pl.when((core == 0) & (s > 0))
    def _():
        greet({"isec": s - 1})

    @pl.when((core == 0) & (s < last))
    def _():
        greet({"isec": s + 1})

    for i in range(user_tiles):
        load_p(i).wait()
        rows = pl.ds(i * TILE, TILE)
        high, low = halves(p_v[rows, :])
        p_hi[rows, :] = high
        p_lo[rows, :] = low
    load_q.wait()
    load_c.wait()

    def errors(visit):
        high, low = halves(q_in[visit])
        q_hi[...] = high
        q_lo[...] = low
        for i in range(user_tiles):
            rows = pl.ds(i * TILE, TILE)
            x = dot3(
                (p_hi[rows, :], p_lo[rows, :]), (q_hi[...], q_lo[...]), ((1,), (1,))
            )
            for j in range(item_tiles):
                k = i * item_tiles + j
                place = jnp.int32(0)
                live = jnp.int32(0)
                for n in range(c_v.shape[1]):
                    hit = (ids_ref[visit, n] == k) & (n < counts_ref[visit])
                    place = place + jnp.where(hit, n, 0)
                    live = live + jnp.where(hit, 1, 0)
                columns = slice(j * TILE, (j + 1) * TILE)
                weight = c_v[visit, place].astype(F32)
                e = jnp.where(live > 0, weight * (x[:, columns] - 1.0), 0.0)
                high, low = halves(e)
                e_hi[rows, pl.ds(j * TILE, TILE)] = high
                e_lo[rows, pl.ds(j * TILE, TILE)] = low
                high, low = halves(e.T)
                et_hi[pl.ds(j * TILE, TILE), rows] = high
                et_lo[pl.ds(j * TILE, TILE), rows] = low

    def item_step(visit):
        for j in range(item_tiles):
            rows = pl.ds(j * TILE, TILE)
            d = dot3(
                (et_hi[rows, :], et_lo[rows, :]), (p_hi[...], p_lo[...]), ((1,), (0,))
            )
            q = q_in[visit, rows, :]
            q_out[visit, rows, :] = q - item_rate * (d + shrinkage * q)

    def user_step(visit):
        for i in range(user_tiles):
            rows = pl.ds(i * TILE, TILE)
            g = dot3(
                (e_hi[rows, :], e_lo[rows, :]), (q_hi[...], q_lo[...]), ((1,), (0,))
            )
            if visit == 0:
                g_v[rows, :] = g
            else:
                g_v[rows, :] = g_v[rows, :] + g

    def near(visit):
        return pltpu.make_async_remote_copy(
            src_ref=q_out.at[visit],
            dst_ref=q_in.at[visit + 1] if visit < VISITS - 1 else items_ref,
            send_sem=near_send.at[visit],
            recv_sem=near_recv.at[visit],
            device_id={"user": nxt if visit < VISITS - 1 else home},
            device_id_type=MESH,
        )

    def piece(way, part):
        return pl.ds(way * chunks * chunk_rows + part * chunk_rows, chunk_rows)

    def hop(visit, way, index, part, arrived=False):
        rows = pl.ds(part * chunk_rows, chunk_rows)
        if arrived:
            source = relay.at[visit, way, index, rows, :]
        elif isinstance(index, int) and index == 0:
            source = q_out.at[visit, piece(way, part), :]
        else:
            source = relay.at[visit, way, index - 1, rows, :]
        return pltpu.make_async_remote_copy(
            src_ref=source,
            dst_ref=relay.at[visit, way, index, rows, :],
            send_sem=far_send.at[visit, way],
            recv_sem=hop_recv.at[visit, way, index, part],
            device_id=chip(column, z + way_step[way], 1),
            device_id_type=MESH,
        )

    def final_hop(visit, way, part):
        rows = pl.ds(part * chunk_rows, chunk_rows)
        landing = q_in.at[visit + 1] if visit < VISITS - 1 else items_ref
        return pltpu.make_async_remote_copy(
            src_ref=relay.at[visit, way, n_isec - 2, rows, :],
            dst_ref=landing.at[piece(way, part), :],
            send_sem=far_send.at[visit, way],
            recv_sem=far_recv.at[visit],
            device_id=relay_target(way, visit),
            device_id_type=MESH,
        )

    def depart(visit):
        for part in range(chunks):
            for way in range(2):
                hop(visit, way, 0, part).start()

    def pass_on(visit, first, end):
        def step(index, carry):
            for part in range(chunks):
                for way in range(2):
                    hop(visit, way, index, part, True).wait_recv()
                    hop(visit, way, index + 1, part).start()
            return carry

        lax.fori_loop(first, end, step, 0)

    def arrive(visit):
        for part in range(chunks):
            for way in range(2):
                hop(visit, way, n_isec - 2, part, True).wait_recv()
                final_hop(visit, way, part).start()

    def whole(source, landing, visit, way):
        return pltpu.make_async_remote_copy(
            src_ref=source,
            dst_ref=landing,
            send_sem=far_send.at[visit, way],
            recv_sem=far_recv.at[visit],
            device_id=chip(column, z + 1, 1),
            device_id_type=MESH,
        )

    def landed(visit):
        landing = q_in.at[visit + 1] if visit < VISITS - 1 else items_ref
        whole(q_out.at[visit], landing, visit, 0).wait_recv()

    def drain_far():
        for visit in range(VISITS):
            for way in range(2):
                hops = relay.at[visit, way]
                whole(hops, hops, visit, way).wait_send()

    def gradient_over(other):
        return pltpu.make_async_remote_copy(
            src_ref=g_v,
            dst_ref=g_peer,
            send_sem=g_send,
            recv_sem=g_recv,
            device_id={"user": other},
            device_id_type=MESH,
        )

    parts = runs.shape[3]
    part_rows = share // parts

    def run_copy(who, way, d, part, source, target):
        return pltpu.make_async_remote_copy(
            src_ref=source,
            dst_ref=runs.at[who, way, d, part],
            send_sem=run_send.at[who],
            recv_sem=run_recv.at[who, way, d, part],
            device_id={"isec": target},
            device_id_type=MESH,
        )

    def shard(ref, d, part):
        start = pl.multiple_of(d * share + part * part_rows, part_rows)
        return ref.at[pl.ds(start, part_rows), :]

    def run_step(who, g_ref, way, d, target, inner, outer, sends):
        @pl.when(inner)
        def _():
            for part in range(parts):
                run = runs.at[who, way, d, part]
                run_copy(who, way, d, part, run, s).wait_recv()

                @pl.when(sends)
                def _():
                    run[...] = run[...] + shard(g_ref, d, part)[...]
                    run_copy(who, way, d, part, run, target).start()

        @pl.when(outer & sends)
        def _():
            for part in range(parts):
                run_copy(who, way, d, part, shard(g_ref, d, part), target).start()

    def line_step(who, g_ref, t):
        d = last + s - t

        @pl.when(t >= s)
        def _():
            run_step(who, g_ref, 0, d, s + 1, s > 0, s == 0, d > s)

        b = t - last + s

        @pl.when(t >= last - s)
        def _():
            run_step(who, g_ref, 1, b, s - 1, s < last, s == last, b < s)

    def line_total(who, g_ref, part):
        mine = shard(g_ref, s, part)[...]
        right = jnp.where(s > 0, runs[who, 0, s, part], 0.0)
        left = jnp.where(s < last, runs[who, 1, s, part], 0.0)
        return mine + (right + left)

    def drain_line(who, g_ref):
        sent = g_ref.at[pl.ds(0, last * share), :]
        pltpu.make_async_remote_copy(
            src_ref=sent,
            dst_ref=sent,
            send_sem=run_send.at[who],
            recv_sem=fin_recv,
            device_id={"isec": lax.rem(s + 1, n_isec)},
            device_id_type=MESH,
        ).wait_send()

    def finish(total, part):
        own = shard(p_v, s, part)[...]
        rows = pl.ds(part * part_rows, part_rows)
        users_ref[rows, :] = own - user_rate * (total + shrinkage * own)

    def finish_copy(other):
        return pltpu.make_async_remote_copy(
            src_ref=fin_out,
            dst_ref=fin_in,
            send_sem=fin_send,
            recv_sem=fin_recv,
            device_id={"user": other},
            device_id_type=MESH,
        )

    errors(0)
    item_step(0)

    @pl.when(core == 0)
    def _():
        greeted = jnp.where(s > 0, 1, 0) + jnp.where(s < last, 1, 0)
        pl.semaphore_wait(barrier, 6 + greeted)
        near(0).start()
        user_step(0)
        for visit in range(1, VISITS - 1):
            landed(visit - 1)
            errors(visit)
            item_step(visit)
            near(visit).start()
            user_step(visit)
        gradient_over(prv).wait_recv()

        def first_steps(t, carry):
            line_step(0, g_peer, t)
            return carry

        def both_steps(t, carry):
            line_step(0, g_peer, t)
            line_step(1, g_v, t - LEAD)
            return carry

        def last_steps(t, carry):
            line_step(1, g_v, t)
            return carry

        lax.fori_loop(0, LEAD, first_steps, 0)
        landed(VISITS - 2)
        errors(VISITS - 1)
        user_step(VISITS - 1)
        item_step(VISITS - 1)
        near(VISITS - 1).start()
        lax.fori_loop(LEAD, n_isec, both_steps, 0)
        for part in range(parts):
            rows = pl.ds(part * part_rows, part_rows)
            fin_out[rows, :] = line_total(0, g_peer, part)
        finish_copy(nxt).start()
        lax.fori_loop(n_isec - LEAD, n_isec, last_steps, 0)
        for part in range(parts):
            finish(line_total(1, g_v, part), part)
        drain_line(0, g_peer)
        drain_line(1, g_v)
        finish_copy(nxt).wait_send()
        for visit in range(VISITS):
            near(visit).wait_send()
        landed(VISITS - 1)

    @pl.when(core == 1)
    def _():
        pl.semaphore_wait(barrier, 8)
        depart(0)
        user_step(0)
        near(0).wait_recv()
        errors(1)
        item_step(1)
        user_step(1)
        pass_on(0, 0, n_isec - 2)
        arrive(0)
        depart(1)
        pass_on(1, 0, 3)
        near(1).wait_recv()
        errors(2)
        pass_on(1, 3, 4)
        item_step(2)
        pass_on(1, 4, 5)
        user_step(2)
        pass_on(1, 5, n_isec - 2)
        arrive(1)
        depart(2)
        pass_on(2, 0, 2)
        near(2).wait_recv()
        errors(3)
        pass_on(2, 2, 3)
        user_step(3)
        gradient_over(prv).start()
        item_step(3)
        pass_on(2, 3, n_isec - 2)
        arrive(2)
        depart(3)
        pass_on(3, 0, n_isec - 2)
        arrive(3)
        gradient_over(prv).wait_send()
        finish_copy(nxt).wait_recv()
        for part in range(parts):
            finish(fin_in[pl.ds(part * part_rows, part_rows), :], part)
        drain_far()
        near(VISITS - 1).wait_recv()


def settle_kernel(users_ref, items_ref, users_out, items_out, users_v, items_v, sem_in, sem_out):
    count = sem_in.shape[0] - 1
    rows = items_v.shape[0] // count

    def moves(users_from, users_to, items_from, items_to, sem):
        yield pltpu.make_async_copy(users_from, users_to, sem.at[count])
        for i in range(count):
            at = pl.ds(i * rows, rows)
            yield pltpu.make_async_copy(items_from.at[at, :], items_to.at[at, :], sem.at[i])

    into = list(moves(users_ref, users_v, items_ref, items_v, sem_in))
    out = list(moves(users_v, users_out, items_v, items_out, sem_out))
    for copy in into:
        copy.start()
    for first, second in zip(into, out):
        first.wait()
        second.start()
    for copy in out:
        copy.wait()


def settle(users, items):
    return pl.pallas_call(
        settle_kernel,
        out_shape=(
            jax.ShapeDtypeStruct(users.shape, F32),
            jax.ShapeDtypeStruct(items.shape, F32),
        ),
        in_specs=[pl.BlockSpec(memory_space=pl.ANY)] * 2,
        out_specs=(pl.BlockSpec(memory_space=pl.ANY),) * 2,
        scratch_shapes=[
            pltpu.VMEM(users.shape, F32),
            pltpu.VMEM(items.shape, F32),
            pltpu.SemaphoreType.DMA((5,)),
            pltpu.SemaphoreType.DMA((5,)),
        ],
        name="settle",
    )(users, items)


def on_device(n_user, n_isec, user_factors, item_factors, confidence, tile_ids, tile_counts):
    user_rows, rank = user_factors.shape
    block = item_factors.shape[0]
    tiles = confidence.shape[3]
    share = user_rows // n_isec
    vmem = functools.partial(pltpu.VMEM, dtype=F32)
    dma = pltpu.SemaphoreType.DMA
    users, items = pl.pallas_call(
        functools.partial(kernel, n_user, n_isec),
        out_shape=(
            jax.ShapeDtypeStruct((share, rank), F32),
            jax.ShapeDtypeStruct((block, rank), F32),
        ),
        in_specs=[pl.BlockSpec(memory_space=pltpu.SMEM)] * 2
        + [pl.BlockSpec(memory_space=pl.ANY)] * 3,
        out_specs=(
            pl.BlockSpec(memory_space=pltpu.VMEM),
            pl.BlockSpec(memory_space=pl.ANY),
        ),
        scratch_shapes=[
            vmem((user_rows, rank)),
            pltpu.VMEM((user_rows, rank), BF16),
            pltpu.VMEM((user_rows, rank), BF16),
            vmem((VISITS, block, rank)),
            vmem((VISITS, block, rank)),
            pltpu.VMEM((block, rank), BF16),
            pltpu.VMEM((block, rank), BF16),
            pltpu.VMEM((VISITS, tiles, TILE, TILE), BF16),
            pltpu.VMEM((block, user_rows), BF16),
            pltpu.VMEM((block, user_rows), BF16),
            pltpu.VMEM((user_rows, block), BF16),
            pltpu.VMEM((user_rows, block), BF16),
            vmem((user_rows, rank)),
            vmem((user_rows, rank)),
            vmem((2, 2, n_isec, PARTS, share // PARTS, rank)),
            vmem((share, rank)),
            vmem((share, rank)),
            vmem((VISITS, 2, n_isec, block // 2, rank)),
            dma((user_rows // TILE + 2,)),
            dma((VISITS,)),
            dma((VISITS,)),
            dma((VISITS, 2)),
            dma((VISITS, 2, n_isec - 1, CHUNKS)),
            dma((VISITS,)),
            dma,
            dma,
            dma((2,)),
            dma((2, 2, n_isec, PARTS)),
            dma,
            dma,
        ],
        compiler_params=pltpu.CompilerParams(
            collective_id=0, has_side_effects=True
        ),
        name="window",
    )(tile_ids[0, 0], tile_counts[0, 0], user_factors, item_factors, confidence[0, 0])
    return settle(users, items)


def solution(mesh):
    sizes = dict(mesh.shape)
    return jax.shard_map(
        functools.partial(on_device, sizes["user"], sizes["isec"]),
        mesh=mesh,
        in_specs=(
            P("user", None),
            P(("user", "isec"), None),
            P("user", "isec", None, None, None, None),
            P("user", "isec", None, None),
            P("user", "isec", None),
        ),
        out_specs=(P(("user", "isec"), None), P(("user", "isec"), None)),
        check_vma=False,
    )
```

time: 171 us -> 141 us (0.82)
  the two profiles are of different devices: /device:TPU:290 before, /device:TPU:1 now
where the time goes in v1:
time: 141 us
  Pallas kernels  140 us (99%)
    pallas_call x1, Pallas kernels, on_device(): pl.pallas_call(functools.partial(kernel, n_user, n_isec), out_shape=(jax....  138 us

profile of v1, /device:TPU:1, one launch (start us, length us, event | category | flops | bytes accessed | tf_op | source)
XLA Modules:
  0.0 140.5 jit_solution(9540128794453340624)
XLA Ops:
  0.6 137.8 %window.1 = (f32[64,512]{1,0:T(8,128)}, f32[256,512]{1,0:T(8,128)}) custom-call(s32[4,6]{1,0:T(4,128)} %bitcast.4, s32[4]{0:T(128)} %bitcast.5, f32[512,512]{1,0:T(8,128)} %p_hbm.1, f32[256,512]{1,0:T(8,128)} %q_hbm.1, bf16[4,6,128,128]{3,2,1,0:T(8,128)(2,1)} %bitcast.3), custom_call_target="tpu_custom_call" | custom-call | tf_op jit(solution)/shard_map/window/pallas_call | solution.py:501
  138.5 1.9 %settle.1 = (f32[64,512]{1,0:T(8,128)}, f32[256,512]{1,0:T(8,128)}) custom-call(f32[64,512]{1,0:T(8,128)} %get-tuple-element.4.users_ref, f32[256,512]{1,0:T(8,128)} %get-tuple-element.5.items_ref), custom_call_target="tpu_custom_call" | custom-call | tf_op jit(solution)/shard_map/settle/pallas_call | solution.py:476

commit v2 on v1

--- a/solution.py
+++ b/solution.py
@@ -11,7 +11,10 @@
 VISITS = 4
 CHUNKS = 4
 PARTS = 2
-LEAD = 3
+LEAD = 4
+PACE = (2, 2)
+STARTS = 2
+STRIDE = 1
 
 item_rate = 0.02
 user_rate = 0.005
@@ -37,8 +40,9 @@
 
 def kernel(
     n_user, n_isec,
-    ids_ref, counts_ref, p_hbm, q_hbm, c_hbm,
+    ids_hbm, counts_hbm, p_hbm, q_hbm, c_hbm,
     users_ref, items_ref,
+    ids_ref, counts_ref,
     p_v, p_hi, p_lo, q_in, q_out, q_hi, q_lo, c_v, et_hi, et_lo, e_hi, e_lo,
     g_v, g_peer, runs, fin_out, fin_in, relay,
     load_sem, near_send, near_recv, far_send, hop_recv, far_recv,
@@ -53,6 +57,8 @@
 
     ring = 2 * n_isec
     chunks = hop_recv.shape[3]
+    hops = hop_recv.shape[2] + 1
+    stride = n_isec // hops
     chunk_rows = block // 2 // chunks
 
     u = lax.axis_index("user")
@@ -64,7 +70,7 @@
     prv = lax.rem(u + n_user - 1, n_user)
     home = lax.rem(u + n_user - (VISITS - 1), n_user)
     guest = lax.rem(u + VISITS - 1, n_user)
-    way_step = (1, ring - 1)
+    way_step = (stride, ring - stride)
 
     def owner(col, z_at, at_core):
         return (col * 2 + z_at // n_isec) * 2 + at_core
@@ -77,7 +83,7 @@
         return 1 if visit < VISITS - 1 else n_user - (VISITS - 1)
 
     def relay_target(way, visit):
-        source = lax.rem(z + (ring - way_step[way]) * (n_isec - 1), ring)
+        source = lax.rem(z + (ring - way_step[way]) * (hops - 1), ring)
         first = owner(column, source, 1)
         return {
             "user": lax.rem(first + shift_of(visit), n_user),
@@ -95,8 +101,15 @@
         rows = pl.ds(i * TILE, TILE)
         return pltpu.make_async_copy(p_hbm.at[rows, :], p_v.at[rows, :], load_sem.at[i])
 
+    load_ids = pltpu.make_async_copy(ids_hbm, ids_ref, load_sem.at[user_tiles + 2])
+    load_counts = pltpu.make_async_copy(
+        counts_hbm, counts_ref, load_sem.at[user_tiles + 3]
+    )
+
     for i in range(user_tiles):
         load_p(i).start()
+    load_ids.start()
+    load_counts.start()
     load_q.start()
     load_c.start()
 
@@ -138,53 +151,74 @@
         p_lo[rows, :] = low
     load_q.wait()
     load_c.wait()
-
-    def errors(visit):
+    load_ids.wait()
+    load_counts.wait()
+
+    def split_items(visit):
         high, low = halves(q_in[visit])
         q_hi[...] = high
         q_lo[...] = low
+
+    def errors_of(visit, i):
+        rows = pl.ds(i * TILE, TILE)
+        x = dot3((p_hi[rows, :], p_lo[rows, :]), (q_hi[...], q_lo[...]), ((1,), (1,)))
+        for j in range(item_tiles):
+            k = i * item_tiles + j
+            place = jnp.int32(0)
+            live = jnp.int32(0)
+            for n in range(c_v.shape[1]):
+                hit = (ids_ref[visit, n] == k) & (n < counts_ref[visit])
+                place = place + jnp.where(hit, n, 0)
+                live = live + jnp.where(hit, 1, 0)
+            columns = slice(j * TILE, (j + 1) * TILE)
+            weight = c_v[visit, place].astype(F32)
+            e = jnp.where(live > 0, weight * (x[:, columns] - 1.0), 0.0)
+            high, low = halves(e)
+            e_hi[rows, pl.ds(j * TILE, TILE)] = high
+            e_lo[rows, pl.ds(j * TILE, TILE)] = low
+            high, low = halves(e.T)
+            et_hi[pl.ds(j * TILE, TILE), rows] = high
+            et_lo[pl.ds(j * TILE, TILE), rows] = low
+
+    def item_step_of(visit, j):
+        rows = pl.ds(j * TILE, TILE)
+        d = dot3(
+            (et_hi[rows, :], et_lo[rows, :]), (p_hi[...], p_lo[...]), ((1,), (0,))
+        )
+        q = q_in[visit, rows, :]
+        q_out[visit, rows, :] = q - item_rate * (d + shrinkage * q)
+
+    def user_step_of(visit, i):
+        rows = pl.ds(i * TILE, TILE)
+        g = dot3(
+            (e_hi[rows, :], e_lo[rows, :]), (q_hi[...], q_lo[...]), ((1,), (0,))
+        )
+        if visit == 0:
+            g_v[rows, :] = g
+        else:
+            g_v[rows, :] = g_v[rows, :] + g
+
+    def errors(visit):
+        split_items(visit)
         for i in range(user_tiles):
-            rows = pl.ds(i * TILE, TILE)
-            x = dot3(
-                (p_hi[rows, :], p_lo[rows, :]), (q_hi[...], q_lo[...]), ((1,), (1,))
-            )
-            for j in range(item_tiles):
-                k = i * item_tiles + j
-                place = jnp.int32(0)
-                live = jnp.int32(0)
-                for n in range(c_v.shape[1]):
-                    hit = (ids_ref[visit, n] == k) & (n < counts_ref[visit])
-                    place = place + jnp.where(hit, n, 0)
-                    live = live + jnp.where(hit, 1, 0)
-                columns = slice(j * TILE, (j + 1) * TILE)
-                weight = c_v[visit, place].astype(F32)
-                e = jnp.where(live > 0, weight * (x[:, columns] - 1.0), 0.0)
-                high, low = halves(e)
-                e_hi[rows, pl.ds(j * TILE, TILE)] = high
-                e_lo[rows, pl.ds(j * TILE, TILE)] = low
-                high, low = halves(e.T)
-                et_hi[pl.ds(j * TILE, TILE), rows] = high
-                et_lo[pl.ds(j * TILE, TILE), rows] = low
+            errors_of(visit, i)
 
     def item_step(visit):
         for j in range(item_tiles):
-            rows = pl.ds(j * TILE, TILE)
-            d = dot3(
-                (et_hi[rows, :], et_lo[rows, :]), (p_hi[...], p_lo[...]), ((1,), (0,))
-            )
-            q = q_in[visit, rows, :]
-            q_out[visit, rows, :] = q - item_rate * (d + shrinkage * q)
+            item_step_of(visit, j)
 
     def user_step(visit):
         for i in range(user_tiles):
-            rows = pl.ds(i * TILE, TILE)
-            g = dot3(
-                (e_hi[rows, :], e_lo[rows, :]), (q_hi[...], q_lo[...]), ((1,), (0,))
-            )
-            if visit == 0:
-                g_v[rows, :] = g
-            else:
-                g_v[rows, :] = g_v[rows, :] + g
+            user_step_of(visit, i)
+
+    def pieces(visit):
+        work = [lambda: near(visit - 1).wait_recv(), lambda: split_items(visit)]
+        work += [functools.partial(errors_of, visit, i) for i in range(user_tiles)]
+        users_part = [functools.partial(user_step_of, visit, i) for i in range(user_tiles)]
+        items_part = [functools.partial(item_step_of, visit, j) for j in range(item_tiles)]
+        if visit < VISITS - 1:
+            return work + items_part + users_part
+        return work + users_part + [lambda: gradient_over(prv).start()] + items_part
 
     def near(visit):
         return pltpu.make_async_remote_copy(
@@ -220,7 +254,7 @@
         rows = pl.ds(part * chunk_rows, chunk_rows)
         landing = q_in.at[visit + 1] if visit < VISITS - 1 else items_ref
         return pltpu.make_async_remote_copy(
-            src_ref=relay.at[visit, way, n_isec - 2, rows, :],
+            src_ref=relay.at[visit, way, hops - 2, rows, :],
             dst_ref=landing.at[piece(way, part), :],
             send_sem=far_send.at[visit, way],
             recv_sem=far_recv.at[visit],
@@ -233,21 +267,36 @@
             for way in range(2):
                 hop(visit, way, 0, part).start()
 
-    def pass_on(visit, first, end):
+    def relay_one(visit, index, part):
+        for way in range(2):
+            hop(visit, way, index, part, True).wait_recv()
+            if isinstance(index, int) and index == hops - 2:
+                final_hop(visit, way, part).start()
+            else:
+                hop(visit, way, index + 1, part).start()
+
+    def cross(visit, starts=None, work=()):
+        depart(visit)
+        work = list(work)
+        if not work:
+            starts = hops - 2
+
         def step(index, carry):
             for part in range(chunks):
-                for way in range(2):
-                    hop(visit, way, index, part, True).wait_recv()
-                    hop(visit, way, index + 1, part).start()
+                relay_one(visit, index, part)
             return carry
 
-        lax.fori_loop(first, end, step, 0)
-
-    def arrive(visit):
-        for part in range(chunks):
-            for way in range(2):
-                hop(visit, way, n_isec - 2, part, True).wait_recv()
-                final_hop(visit, way, part).start()
+        if starts > 0:
+            lax.fori_loop(0, starts, step, 0)
+        for index in range(starts, hops - 1):
+            left = (PACE[0] if index == starts else PACE[1]) if work else 0
+            for part in range(chunks):
+                relay_one(visit, index, part)
+                for _ in range(left):
+                    if work:
+                        work.pop(0)()
+        for piece_of_work in work:
+            piece_of_work()
 
     def whole(source, landing, visit, way):
         return pltpu.make_async_remote_copy(
@@ -266,8 +315,8 @@
     def drain_far():
         for visit in range(VISITS):
             for way in range(2):
-                hops = relay.at[visit, way]
-                whole(hops, hops, visit, way).wait_send()
+                slots = relay.at[visit, way]
+                whole(slots, slots, visit, way).wait_send()
 
     def gradient_over(other):
         return pltpu.make_async_remote_copy(
@@ -412,83 +461,17 @@
     @pl.when(core == 1)
     def _():
         pl.semaphore_wait(barrier, 8)
-        depart(0)
-        user_step(0)
-        near(0).wait_recv()
-        errors(1)
-        item_step(1)
-        user_step(1)
-        pass_on(0, 0, n_isec - 2)
-        arrive(0)
-        depart(1)
-        pass_on(1, 0, 3)
-        near(1).wait_recv()
-        errors(2)
-        pass_on(1, 3, 4)
-        item_step(2)
-        pass_on(1, 4, 5)
-        user_step(2)
-        pass_on(1, 5, n_isec - 2)
-        arrive(1)
-        depart(2)
-        pass_on(2, 0, 2)
-        near(2).wait_recv()
-        errors(3)
-        pass_on(2, 2, 3)
-        user_step(3)
-        gradient_over(prv).start()
-        item_step(3)
-        pass_on(2, 3, n_isec - 2)
-        arrive(2)
-        depart(3)
-        pass_on(3, 0, n_isec - 2)
-        arrive(3)
+        first = [functools.partial(user_step_of, 0, i) for i in range(user_tiles)]
+        cross(0, 0, first + pieces(1))
+        cross(1, STARTS, pieces(2))
+        cross(2, STARTS, pieces(3))
+        cross(3)
         gradient_over(prv).wait_send()
         finish_copy(nxt).wait_recv()
         for part in range(parts):
             finish(fin_in[pl.ds(part * part_rows, part_rows), :], part)
         drain_far()
         near(VISITS - 1).wait_recv()
-
-
-def settle_kernel(users_ref, items_ref, users_out, items_out, users_v, items_v, sem_in, sem_out):
-    count = sem_in.shape[0] - 1
-    rows = items_v.shape[0] // count
-
-    def moves(users_from, users_to, items_from, items_to, sem):
-        yield pltpu.make_async_copy(users_from, users_to, sem.at[count])
-        for i in range(count):
-            at = pl.ds(i * rows, rows)
-            yield pltpu.make_async_copy(items_from.at[at, :], items_to.at[at, :], sem.at[i])
-
-    into = list(moves(users_ref, users_v, items_ref, items_v, sem_in))
-    out = list(moves(users_v, users_out, items_v, items_out, sem_out))
-    for copy in into:
-        copy.start()
-    for first, second in zip(into, out):
-        first.wait()
-        second.start()
-    for copy in out:
-        copy.wait()
-
-
-def settle(users, items):
-    return pl.pallas_call(
-        settle_kernel,
-        out_shape=(
-            jax.ShapeDtypeStruct(users.shape, F32),
-            jax.ShapeDtypeStruct(items.shape, F32),
-        ),
-        in_specs=[pl.BlockSpec(memory_space=pl.ANY)] * 2,
-        out_specs=(pl.BlockSpec(memory_space=pl.ANY),) * 2,
-        scratch_shapes=[
-            pltpu.VMEM(users.shape, F32),
-            pltpu.VMEM(items.shape, F32),
-            pltpu.SemaphoreType.DMA((5,)),
-            pltpu.SemaphoreType.DMA((5,)),
-        ],
-        name="settle",
-    )(users, items)
 
 
 def on_device(n_user, n_isec, user_factors, item_factors, confidence, tile_ids, tile_counts):
@@ -498,19 +481,14 @@
     share = user_rows // n_isec
     vmem = functools.partial(pltpu.VMEM, dtype=F32)
     dma = pltpu.SemaphoreType.DMA
-    users, items = pl.pallas_call(
+    return pl.pallas_call(
         functools.partial(kernel, n_user, n_isec),
-        out_shape=(
-            jax.ShapeDtypeStruct((share, rank), F32),
-            jax.ShapeDtypeStruct((block, rank), F32),
-        ),
-        in_specs=[pl.BlockSpec(memory_space=pltpu.SMEM)] * 2
-        + [pl.BlockSpec(memory_space=pl.ANY)] * 3,
-        out_specs=(
-            pl.BlockSpec(memory_space=pltpu.VMEM),
-            pl.BlockSpec(memory_space=pl.ANY),
-        ),
+        out_shape=(vmem((share, rank)), vmem((block, rank))),
+        in_specs=[pl.BlockSpec(memory_space=pl.ANY)] * 5,
+        out_specs=(pl.BlockSpec(memory_space=pltpu.VMEM),) * 2,
         scratch_shapes=[
+            pltpu.SMEM((VISITS, tiles), jnp.int32),
+            pltpu.SMEM((VISITS,), jnp.int32),
             vmem((user_rows, rank)),
             pltpu.VMEM((user_rows, rank), BF16),
             pltpu.VMEM((user_rows, rank), BF16),
@@ -528,12 +506,12 @@
             vmem((2, 2, n_isec, PARTS, share // PARTS, rank)),
             vmem((share, rank)),
             vmem((share, rank)),
-            vmem((VISITS, 2, n_isec, block // 2, rank)),
-            dma((user_rows // TILE + 2,)),
+            vmem((VISITS, 2, n_isec // STRIDE, block // 2, rank)),
+            dma((user_rows // TILE + 4,)),
             dma((VISITS,)),
             dma((VISITS,)),
             dma((VISITS, 2)),
-            dma((VISITS, 2, n_isec - 1, CHUNKS)),
+            dma((VISITS, 2, n_isec // STRIDE - 1, CHUNKS)),
             dma((VISITS,)),
             dma,
             dma,
@@ -547,7 +525,6 @@
         ),
         name="window",
     )(tile_ids[0, 0], tile_counts[0, 0], user_factors, item_factors, confidence[0, 0])
-    return settle(users, items)
 
 
 def solution(mesh):

time: 141 us -> 136 us (0.965)
  Pallas kernels: 140 us -> 133 us
  local copies, waits for them, and re-layouts: 0 us -> 1.45 us
    pallas_call x2 -> x1, Pallas kernels: 140 us -> 133 us  [on_device(): pl.pallas_call(functools.partial(kernel, n_user, n_isec), out_shape=(vmem...]
    unnamed x0 -> x2, local copies, waits for them, and re-layouts: none -> 1.45 us
where the time goes in v2:
time: 136 us; the launch traced here: 135 us
  Pallas kernels  133 us (98%)
  local copies, waits for them, and re-layouts  1.45 us (1%)
    pallas_call x1, Pallas kernels, on_device(): pl.pallas_call(functools.partial(kernel, n_user, n_isec), out_shape=(vmem...  133 us

profile of v2, /device:TPU:1, one launch (start us, length us, event | category | flops | bytes accessed | tf_op | source)
XLA Modules:
  0.0 135.4 jit_solution(1574284563796557440)
XLA Ops:
  0.6 133.3 %window.1 = (f32[64,512]{1,0:T(8,128)S(1)}, f32[256,512]{1,0:T(8,128)S(1)}) custom-call(s32[4,6]{1,0:T(4,128)} %bitcast.4, s32[4]{0:T(128)} %bitcast.5, f32[512,512]{1,0:T(8,128)} %p_hbm.1, f32[256,512]{1,0:T(8,128)} %q_hbm.1, bf16[4,6,128,128]{3,2,1,0:T(8,128)(2,1)} %bitcast.3), custom_call_target="tpu_custom_call" | custom-call | tf_op jit(solution)/shard_map/window/pallas_call | solution.py:484
  133.9 0.7 copy.9
  134.6 0.8 copy.10

commit v3 on v2

--- a/solution.py
+++ b/solution.py
@@ -56,8 +56,8 @@
     last = n_isec - 1
 
     ring = 2 * n_isec
-    chunks = hop_recv.shape[3]
-    hops = hop_recv.shape[2] + 1
+    chunks = hop_recv.shape[2]
+    hops = hop_recv.shape[1] + 1
     stride = n_isec // hops
     chunk_rows = block // 2 // chunks
 
@@ -245,7 +245,7 @@
             src_ref=source,
             dst_ref=relay.at[visit, way, index, rows, :],
             send_sem=far_send.at[visit, way],
-            recv_sem=hop_recv.at[visit, way, index, part],
+            recv_sem=hop_recv.at[visit, index, part],
             device_id=chip(column, z + way_step[way], 1),
             device_id_type=MESH,
         )
@@ -268,8 +268,16 @@
                 hop(visit, way, 0, part).start()
 
     def relay_one(visit, index, part):
+        both = relay.at[visit, :, index, pl.ds(part * chunk_rows, chunk_rows), :]
+        pltpu.make_async_remote_copy(
+            src_ref=both,
+            dst_ref=both,
+            send_sem=far_send.at[visit, 0],
+            recv_sem=hop_recv.at[visit, index, part],
+            device_id=chip(column, z + 1, 1),
+            device_id_type=MESH,
+        ).wait_recv()
         for way in range(2):
-            hop(visit, way, index, part, True).wait_recv()
             if isinstance(index, int) and index == hops - 2:
                 final_hop(visit, way, part).start()
             else:
@@ -345,35 +353,34 @@
         start = pl.multiple_of(d * share + part * part_rows, part_rows)
         return ref.at[pl.ds(start, part_rows), :]
 
-    def run_step(who, g_ref, way, d, target, inner, outer, sends):
+    def run_step(who, g_ref, way, d, part, target, inner, outer, sends):
+        run = runs.at[who, way, d, part]
+
         @pl.when(inner)
         def _():
-            for part in range(parts):
-                run = runs.at[who, way, d, part]
-                run_copy(who, way, d, part, run, s).wait_recv()
-
-                @pl.when(sends)
-                def _():
-                    run[...] = run[...] + shard(g_ref, d, part)[...]
-                    run_copy(who, way, d, part, run, target).start()
+            run_copy(who, way, d, part, run, s).wait_recv()
+
+            @pl.when(sends)
+            def _():
+                run[...] = run[...] + shard(g_ref, d, part)[...]
+                run_copy(who, way, d, part, run, target).start()
 
         @pl.when(outer & sends)
         def _():
-            for part in range(parts):
-                run_copy(who, way, d, part, shard(g_ref, d, part), target).start()
-
-    def line_step(who, g_ref, t):
+            run_copy(who, way, d, part, shard(g_ref, d, part), target).start()
+
+    def line_step(who, g_ref, t, part):
         d = last + s - t
 
         @pl.when(t >= s)
         def _():
-            run_step(who, g_ref, 0, d, s + 1, s > 0, s == 0, d > s)
+            run_step(who, g_ref, 0, d, part, s + 1, s > 0, s == 0, d > s)
 
         b = t - last + s
 
         @pl.when(t >= last - s)
         def _():
-            run_step(who, g_ref, 1, b, s - 1, s < last, s == last, b < s)
+            run_step(who, g_ref, 1, b, part, s - 1, s < last, s == last, b < s)
 
     def line_total(who, g_ref, part):
         mine = shard(g_ref, s, part)[...]
@@ -425,16 +432,19 @@
         gradient_over(prv).wait_recv()
 
         def first_steps(t, carry):
-            line_step(0, g_peer, t)
+            for part in range(parts):
+                line_step(0, g_peer, t, part)
             return carry
 
         def both_steps(t, carry):
-            line_step(0, g_peer, t)
-            line_step(1, g_v, t - LEAD)
+            for part in range(parts):
+                line_step(0, g_peer, t, part)
+                line_step(1, g_v, t - LEAD, part)
             return carry
 
         def last_steps(t, carry):
-            line_step(1, g_v, t)
+            for part in range(parts):
+                line_step(1, g_v, t, part)
             return carry
 
         lax.fori_loop(0, LEAD, first_steps, 0)
@@ -511,7 +521,7 @@
             dma((VISITS,)),
             dma((VISITS,)),
             dma((VISITS, 2)),
-            dma((VISITS, 2, n_isec // STRIDE - 1, CHUNKS)),
+            dma((VISITS, n_isec // STRIDE - 1, CHUNKS)),
             dma((VISITS,)),
             dma,
             dma,

time: 136 us -> 135 us (level)
  no operation moved by 1% of the time
where the time goes in v3:
time: 135 us
  Pallas kernels  133 us (99%)
  local copies, waits for them, and re-layouts  1.45 us (1%)
    pallas_call x1, Pallas kernels, on_device(): pl.pallas_call(functools.partial(kernel, n_user, n_isec), out_shape=(vmem...  133 us

profile of v3, /device:TPU:1, one launch (start us, length us, event | category | flops | bytes accessed | tf_op | source)
XLA Modules:
  0.0 135.0 jit_solution(9043310113239254070)
XLA Ops:
  0.6 132.9 %window.1 = (f32[64,512]{1,0:T(8,128)S(1)}, f32[256,512]{1,0:T(8,128)S(1)}) custom-call(s32[4,6]{1,0:T(4,128)} %bitcast.4, s32[4]{0:T(128)} %bitcast.5, f32[512,512]{1,0:T(8,128)} %p_hbm.1, f32[256,512]{1,0:T(8,128)} %q_hbm.1, bf16[4,6,128,128]{3,2,1,0:T(8,128)(2,1)} %bitcast.3), custom_call_target="tpu_custom_call" | custom-call | tf_op jit(solution)/shard_map/window/pallas_call | solution.py:494
  133.5 0.7 copy.9
  134.2 0.8 copy.10

commit v4 on v3

--- a/solution.py
+++ b/solution.py
@@ -12,7 +12,7 @@
 CHUNKS = 4
 PARTS = 2
 LEAD = 4
-PACE = (2, 2)
+PACE = (1, 2)
 STARTS = 2
 STRIDE = 1
 

time: 135 us -> 135 us (level)
  no operation moved by 1% of the time
where the time goes in v4:
time: 135 us
  Pallas kernels  133 us (99%)
  local copies, waits for them, and re-layouts  1.45 us (1%)
    pallas_call x1, Pallas kernels, on_device(): pl.pallas_call(functools.partial(kernel, n_user, n_isec), out_shape=(vmem...  133 us

profile of v4, /device:TPU:1, one launch (start us, length us, event | category | flops | bytes accessed | tf_op | source)
XLA Modules:
  0.0 135.0 jit_solution(5753465898100216050)
XLA Ops:
  0.6 132.9 %window.1 = (f32[64,512]{1,0:T(8,128)S(1)}, f32[256,512]{1,0:T(8,128)S(1)}) custom-call(s32[4,6]{1,0:T(4,128)} %bitcast.4, s32[4]{0:T(128)} %bitcast.5, f32[512,512]{1,0:T(8,128)} %p_hbm.1, f32[256,512]{1,0:T(8,128)} %q_hbm.1, bf16[4,6,128,128]{3,2,1,0:T(8,128)(2,1)} %bitcast.3), custom_call_target="tpu_custom_call" | custom-call | tf_op jit(solution)/shard_map/window/pallas_call | solution.py:494
  133.5 0.7 copy.9
  134.2 0.8 copy.10
